TPU v7x, 32 devices: a whole 2x2x4 slice. The times are simulated.
32 devices in a mesh: dp: 2 (over x), expert: 16 (over z, y, core).
Axes of the slice: x: 2, y: 2, z: 4, core: 2. Of those that a mesh axis runs over, the one named last changes fastest.
Arguments:
- tokens: bfloat16 [4096, 1792], P(('dp', 'expert')), may hold values from -6 to 6
- routes: int32 [4096, 4], P(('dp', 'expert')), may hold values from 0 to 15, all different within a row; in each aligned block of 128 rows (0 to 127, 128 to 255, ...) at most 64 rows name the same one
- route_weight: float32 [4096, 4], P(('dp', 'expert')), may hold values from 0.1 to 1
- w_in: float32 [16, 2, 1792, 1280], P('expert', None, 'dp'), may hold values from -0.125 to 0.125
- m_in: float32 [16, 2, 1792, 1280], P('expert', None, 'dp'), may hold values from -6 to 6
- v_in: float32 [16, 2, 1792, 1280], P('expert', None, 'dp'), may hold values from 0.5 to 20
- g_in: bfloat16 [16, 2, 1792, 1280], P('expert', None, 'dp'), may hold values from -30 to 30
- w_out: float32 [16, 1280, 1792], P('expert', 'dp'), may hold values from -0.15625 to 0.15625
- m_out: float32 [16, 1280, 1792], P('expert', 'dp'), may hold values from -6 to 6
- v_out: float32 [16, 1280, 1792], P('expert', 'dp'), may hold values from 0.5 to 20
- g_out: bfloat16 [16, 1280, 1792], P('expert', 'dp'), may hold values from -30 to 30
Outputs:
- mixed: bfloat16 [4096, 1792], P(('dp', 'expert'))
Inputs may be any that keep to these rules, and one draw needn't show every extreme that they name: `routes`: A token's 4 experts differ. Within the rows of one device (aligned blocks of 128 tokens) each expert is named at most 64 times, a bound that some block reaches.
All inputs are finite; a program needn't handle non-finite values.
Results may differ from a plain program's by a relative error of at most 0.008.
Values may be sent and summed in bfloat16 or wider, within the bound.
No kernel may reach another device: no remote copies, remote signals or barrier semaphores. Data moves between devices by JAX's collectives and lax.ppermute only.
A program may use at most 128 MiB of HBM per device.

v0:
```python
import jax
import jax.numpy as jnp
from jax import lax
from jax.sharding import PartitionSpec as P

beta_one = 0.9
beta_two = 0.95
corr_one = 0.99997343860111
corr_two = 0.99407947077967
adam_eps = 1e-08
learn_rate = 0.01
weight_decay = 0.1


def adamw(master, moment, second, gradient):
    grad_value = gradient.astype(jnp.float32)
    moment_new = beta_one * moment + (1.0 - beta_one) * grad_value
    second_new = beta_two * second + (1.0 - beta_two) * grad_value * grad_value
    update = moment_new / corr_one / (jnp.sqrt(second_new / corr_two) + adam_eps)
    return (master - learn_rate * (update + weight_decay * master)).astype(jnp.bfloat16)


def expert_apply(block_rows, gate_up, down_proj):
    gate_pre = jnp.dot(block_rows, gate_up[0], preferred_element_type=jnp.float32)
    up_pre = jnp.dot(block_rows, gate_up[1], preferred_element_type=jnp.float32)
    hidden = (jax.nn.silu(gate_pre) * up_pre).astype(jnp.bfloat16)
    return jnp.dot(hidden, down_proj, preferred_element_type=jnp.float32).astype(jnp.bfloat16)


def per_device(tokens, routes, route_weight, w_in, m_in, v_in, g_in, w_out, m_out, v_out, g_out):
    groups = lax.axis_size("expert")
    tok_rows, width = tokens.shape
    top_count = routes.shape[1]
    capacity = 2 * tok_rows * top_count // groups
    slot_total = groups * capacity
    flat_routes = routes.reshape(-1)
    owners = jnp.arange(tok_rows * top_count, dtype=jnp.int32) // top_count
    onehot = (flat_routes[:, None] == jnp.arange(groups, dtype=jnp.int32)[None, :]).astype(
        jnp.int32
    )
    earlier = jnp.cumsum(onehot, axis=0) - onehot
    slot_ids = flat_routes * capacity + jnp.sum(earlier * onehot, axis=1)
    matches = (jnp.arange(slot_total, dtype=jnp.int32)[:, None] == slot_ids[None, :]).astype(
        jnp.int32
    )
    live_flags = jnp.sum(matches, axis=1)
    sources = jnp.sum(matches * owners[None, :], axis=1)
    outgoing = jnp.where(
        live_flags[:, None] > 0, jnp.take(tokens, sources, axis=0), jnp.zeros((), jnp.bfloat16)
    )
    outgoing = outgoing.reshape(groups, capacity, width)
    gate_up_own = adamw(w_in, m_in, v_in, g_in)
    down_own = adamw(w_out, m_out, v_out, g_out)
    gate_up_all, down_all = (
        lax.all_gather(gate_up_own, "dp", axis=2, tiled=True),
        lax.all_gather(down_own, "dp", axis=1, tiled=True),
    )
    gate_up_all = gate_up_all[0]
    down_all = down_all[0]
    arrived = lax.all_to_all(outgoing, "expert", split_axis=0, concat_axis=0, tiled=True)
    src_count, item_count, depth = arrived.shape
    results = expert_apply(arrived.reshape(src_count * item_count, depth), gate_up_all, down_all)
    returned = lax.all_to_all(
        results.reshape(src_count, item_count, depth),
        "expert",
        split_axis=0,
        concat_axis=0,
        tiled=True,
    )
    back_rows = returned.reshape(slot_total, width)
    picked = jnp.take(back_rows, slot_ids, axis=0).reshape(tok_rows, top_count, width)
    mixed = jnp.einsum("tkd,tk->td", picked.astype(jnp.float32), route_weight)
    return mixed.astype(jnp.bfloat16)


def solution(mesh):
    placed = (
        P(("dp", "expert"), None),
        P(("dp", "expert"), None),
        P(("dp", "expert"), None),
        P("expert", None, "dp", None),
        P("expert", None, "dp", None),
        P("expert", None, "dp", None),
        P("expert", None, "dp", None),
        P("expert", "dp", None),
        P("expert", "dp", None),
        P("expert", "dp", None),
        P("expert", "dp", None),
    )
    return jax.shard_map(
        per_device, mesh=mesh, in_specs=placed, out_specs=P(("dp", "expert"), None), check_vma=False
    )
```

profile of v0, /device:TPU:13, one launch (start us, length us, event | category | flops | bytes accessed | tf_op | source)
XLA Modules:
  0.0 321.8 jit_solution(14130354213369942795)
XLA Ops:
  6.5 15.8 %fusion.10 = bf16[1,2,896,1280]{3,2,1,0:T(8,128)(2,1)} fusion(f32[1,2,896,1280]{3,2,1,0:T(8,128)} %param.14, f32[1,2,896,1280]{3,2,1,0:T(8,128)} %param.16, bf16[1,2,896,1280]{3,2,1,0:T(8,128)(2,1)} %param.17, f32[1,2,896,1280]{3,2,1,0:T(8,128)} %param.15), kind=kLoop, calls=%fused_computation.14 | loop fusion | flops 38993920 | bytes 36700160 | tf_op jit(solution)/shard_map/convert_element_type | solution.py:20
  22.4 0.7 copy-done.3
  23.4 1.2 reduce-window.6
  24.6 0.2 slice_reduce_fusion
  24.9 0.6 convert_reduce_fusion
  25.8 5.8 %gather_fusion = bf16[1024,1792]{1,0:T(8,128)(2,1)} fusion(bf16[128,1792]{1,0:T(8,128)(2,1)S(1)} %copy-done, s32[1024]{0:T(1024)S(1)} %broadcast_clamp_fusion), kind=kCustom, calls=%fused_computation | custom fusion | bytes 7344128 | tf_op jit(solution)/shard_map/jit(_take)/gather | solution.py:49
  31.6 4.7 %select_select_fusion = bf16[16,64,1792]{2,1,0:T(8,128)(2,1)} fusion(bf16[16,64,1792]{2,1,0:T(8,128)(2,1)} %bitcast.47, pred[16,64]{1,0:T(8,128)(4,1)S(1)} %compare_and_fusion, pred[16,64]{1,0:T(8,128)(4,1)S(1)} %gt.20), kind=kLoop, calls=%fused_computation.35 | loop fusion | flops 3670016 | bytes 7342080 | tf_op jit(solution)/shard_map/jit(_where)/select_n | solution.py:48
  36.3 6.7 %all-to-all-start = ((bf16[16,64,1792]{2,1,0:T(8,128)(2,1)}), bf16[16,64,1792]{2,1,0:T(8,128)(2,1)}, u32[]{:S(2)}, u32[]{:S(2)}) async-start(bf16[16,64,1792]{2,1,0:T(8,128)(2,1)} %select_select_fusion), calls=%async_computation | async-start | bytes 7340032 | tf_op jit(solution)/shard_map/all_to_all | solution.py:60
  43.1 0.2 all-gather.5.cloned.1.call-start
  43.3 7.9 %fusion.24 = bf16[1,640,1792]{2,1,0:T(8,128)(2,1)} fusion(f32[1,640,1792]{2,1,0:T(8,128)} %param.18, f32[1,640,1792]{2,1,0:T(8,128)} %param.20, bf16[1,640,1792]{2,1,0:T(8,128)(2,1)S(1)} %copy-done.2, f32[1,640,1792]{2,1,0:T(8,128)} %param.19), kind=kLoop, calls=%fused_computation.33 | loop fusion | flops 19496960 | bytes 18350080 | tf_op jit(solution)/shard_map/convert_element_type | solution.py:20
  51.3 73.3 %all-to-all-done = bf16[16,64,1792]{2,1,0:T(8,128)(2,1)} async-done(((bf16[16,64,1792]{2,1,0:T(8,128)(2,1)}), bf16[16,64,1792]{2,1,0:T(8,128)(2,1)}, u32[]{:S(2)}, u32[]{:S(2)}) %all-to-all-start) | async-done | bytes 3670048 | tf_op jit(solution)/shard_map/all_to_all | solution.py:60
  124.6 12.0 %all-gather.3.cloned.1.call-done = bf16[1,2,1792,1280]{3,2,1,0:T(8,128)(2,1)} async-done(((bf16[1,2,896,1280]{3,2,1,0:T(8,128)(2,1)}), bf16[1,2,1792,1280]{3,2,1,0:T(8,128)(2,1)}) %all-gather.3.cloned.1.call-update) | async-done | bytes 9175056 | tf_op jit(solution)/shard_map/all_gather | solution.py:55
  136.5 11.0 %fusion.21 = f32[1024,1280]{1,0:T(8,128)} fusion(bf16[1024,1792]{1,0:T(8,128)(2,1)} %bitcast.4, bf16[1,2,1792,1280]{3,2,1,0:T(8,128)(2,1)} %all-gather.3.cloned.1.call-done), kind=kOutput, calls=%fused_computation.30 | convolution fusion | flops 4697620480 | bytes 13500416 | tf_op jit(solution)/shard_map/dot_general | solution.py:24
  147.5 51.8 %all-gather.5.cloned.1.call-done = bf16[1,1280,1792]{2,1,0:T(8,128)(2,1)} async-done(((bf16[1,640,1792]{2,1,0:T(8,128)(2,1)}), bf16[1,1280,1792]{2,1,0:T(8,128)(2,1)}) %all-gather.5.cloned.1.call-update) | async-done | bytes 4587536 | tf_op jit(solution)/shard_map/all_gather | solution.py:56
  199.3 16.4 %fusion.25 = bf16[1024,1792]{1,0:T(8,128)(2,1)} fusion(bf16[1,1280,1792]{2,1,0:T(8,128)(2,1)} %all-gather.5.cloned.1.call-done, f32[1024,1280]{1,0:T(8,128)} %fusion.21, bf16[1024,1792]{1,0:T(8,128)(2,1)} %bitcast.4, bf16[1,2,1792,1280]{3,2,1,0:T(8,128)(2,1)} %all-gather.3.cloned.1.call-done), kind=kOutput, calls=%fused_computation.34 | convolution fusion | flops 9404940288 | bytes 21757952 | tf_op jit(solution)/shard_map/dot_general | solution.py:27
  215.6 6.6 %all-to-all-start.1 = ((bf16[16,64,1792]{2,1,0:T(8,128)(2,1)}), bf16[16,64,1792]{2,1,0:T(8,128)(2,1)}, u32[]{:S(2)}, u32[]{:S(2)}) async-start(bf16[16,64,1792]{2,1,0:T(8,128)(2,1)} %bitcast.48), calls=%async_computation.1 | async-start | bytes 7340032 | tf_op jit(solution)/shard_map/all_to_all | solution.py:63
  222.4 0.1 copy.26
  222.7 0.1 copy.25
  222.9 0.2 copy.27
  223.1 80.5 %all-to-all-done.1 = bf16[16,64,1792]{2,1,0:T(8,128)(2,1)} async-done(((bf16[16,64,1792]{2,1,0:T(8,128)(2,1)}), bf16[16,64,1792]{2,1,0:T(8,128)(2,1)}, u32[]{:S(2)}, u32[]{:S(2)}) %all-to-all-start.1) | async-done | bytes 3670048 | tf_op jit(solution)/shard_map/all_to_all | solution.py:63
  303.5 6.5 %gather_fusion.1 = bf16[512,1792]{1,0:T(8,128)(2,1)S(1)} fusion(bf16[1024,1792]{1,0:T(8,128)(2,1)} %bitcast.9, s32[1024]{0:T(1024)S(1)} %pad_clamp_fusion), kind=kCustom, calls=%fused_computation.1 | custom fusion | bytes 3672064 | tf_op jit(solution)/shard_map/jit(_take)/gather | solution.py:71
  310.0 1.5 gather.15
  311.5 2.7 fusion.28
  314.2 0.8 copy.32
  (33 shorter events, 1.0 us)
Async XLA Ops:
  6.5 19.2 %copy-start = (bf16[128,1792]{1,0:T(8,128)(2,1)S(1)}, bf16[128,1792]{1,0:T(8,128)(2,1)}, u32[]{:S(2)}) copy-start(bf16[128,1792]{1,0:T(8,128)(2,1)} %param.11) | copy-start | bytes 1376260
  6.5 130.0 %all-gather.3.cloned.1.call-start = ((), (), s32[]{:S(2)}) async-start(), calls=%async_computation.2 | async-start | bytes 13762560 | tf_op jit(solution)/shard_map/all_gather | solution.py:55
  22.4 0.7 copy-start.3
  36.3 7.0 %copy-start.2 = (bf16[1,640,1792]{2,1,0:T(8,128)(2,1)S(1)}, bf16[1,640,1792]{2,1,0:T(8,128)(2,1)}, u32[]{:S(2)}) copy-start(bf16[1,640,1792]{2,1,0:T(8,128)(2,1)} %param.21) | copy-start | bytes 6881284
  36.3 88.3 %all-to-all-start = ((bf16[16,64,1792]{2,1,0:T(8,128)(2,1)}), bf16[16,64,1792]{2,1,0:T(8,128)(2,1)}, u32[]{:S(2)}, u32[]{:S(2)}) async-start(bf16[16,64,1792]{2,1,0:T(8,128)(2,1)} %select_select_fusion), calls=%async_computation | async-start | bytes 7340032 | tf_op jit(solution)/shard_map/all_to_all | solution.py:60
  43.1 156.2 %all-gather.5.cloned.1.call-start = ((), (), s32[]{:S(2)}) async-start(), calls=%async_computation.3 | async-start | bytes 6881280 | tf_op jit(solution)/shard_map/all_gather | solution.py:56
  215.6 7.2 %copy-start.4 = (f32[128,4]{0,1:T(4,128)S(1)}, f32[128,4]{0,1:T(4,128)}, u32[]{:S(2)}) copy-start(f32[128,4]{0,1:T(4,128)} %param.13) | copy-start | bytes 6148
  215.6 87.9 %all-to-all-start.1 = ((bf16[16,64,1792]{2,1,0:T(8,128)(2,1)}), bf16[16,64,1792]{2,1,0:T(8,128)(2,1)}, u32[]{:S(2)}, u32[]{:S(2)}) async-start(bf16[16,64,1792]{2,1,0:T(8,128)(2,1)} %bitcast.48), calls=%async_computation.1 | async-start | bytes 7340032 | tf_op jit(solution)/shard_map/all_to_all | solution.py:63
  310.0 5.0 %copy-start.1 = (bf16[128,1792]{1,0:T(8,128)(2,1)S(1)}, bf16[128,1792]{1,0:T(8,128)(2,1)}, u32[]{:S(2)}) copy-start(bf16[128,1792]{1,0:T(8,128)(2,1)} %param.11) | copy-start | bytes 1376260
Sparse Core Ops, SparseCore 0:
  22.5 113.9 all-gather.2
  138.1 61.1 all-gather.4
where the time goes:
time: 322 us
  waiting for transfers between devices  218 us (68%)
  other arithmetic  30.5 us (9%)
  matrix products  30 us (9%)
  local copies, waits for them, and re-layouts  16.6 us (5%)
  starting transfers between devices  13.6 us (4%)
  between operations  13.5 us (4%)
    all_to_all x1, waiting for transfers between devices, per_device(): lax.all_to_all(results.reshape(src_count, item_count, depth), 'expert', s...  80.5 us
    all_to_all x1, waiting for transfers between devices, per_device(): lax.all_to_all(outgoing, 'expert', split_axis=0, concat_axis=0, tiled=True)  73.3 us
    all_gather x1, waiting for transfers between devices, per_device(): lax.all_gather(down_own, 'dp', axis=1, tiled=True)  51.8 us
    convert_element_type x2, other arithmetic, adamw(): (master - learn_rate * (update + weight_decay * master)).astype(jnp.bfloa...  23.8 us
    dot_general x1, matrix products, expert_apply(): jnp.dot(hidden, down_proj, preferred_element_type=jnp.float32)  16.4 us
    all_gather x1, waiting for transfers between devices, per_device(): lax.all_gather(gate_up_own, 'dp', axis=2, tiled=True)  12 us
    dot_general x1, matrix products, expert_apply(): jnp.dot(block_rows, gate_up[0], preferred_element_type=jnp.float32)  11 us
    gather x2, local copies, waits for them, and re-layouts, per_device(): jnp.take(back_rows, slot_ids, axis=0).reshape(tok_rows, top_count, width)  7.94 us
  transfers between devices with their start and end apart: 4, of which 4 were waited for; matrix products, arithmetic and copies ran while one was open for 10% of the time, Pallas kernels for 0%

commit v1 on v0

--- a/solution.py
+++ b/solution.py
@@ -10,6 +10,13 @@
 adam_eps = 1e-08
 learn_rate = 0.01
 weight_decay = 0.1
+
+
+def swapped_in(x, axis, d):
+    size = lax.axis_size(axis)
+    tiles = jnp.stack([x for _ in range(size)])
+    tiles = lax.all_to_all(tiles, axis, split_axis=0, concat_axis=0)
+    return jnp.concatenate(tiles, axis=d)
 
 
 def adamw(master, moment, second, gradient):
@@ -53,7 +60,7 @@
     down_own = adamw(w_out, m_out, v_out, g_out)
     gate_up_all, down_all = (
         lax.all_gather(gate_up_own, "dp", axis=2, tiled=True),
-        lax.all_gather(down_own, "dp", axis=1, tiled=True),
+        swapped_in(down_own, "dp", 1),
     )
     gate_up_all = gate_up_all[0]
     down_all = down_all[0]

time: 322 us -> 308 us (0.957)
  waiting for transfers between devices: 218 us -> 197 us
  starting transfers between devices: 13.6 us -> 18.9 us
    all_gather x1 -> x0, waiting for transfers between devices: 51.8 us -> none  [per_device(): lax.all_gather(down_own, 'dp', axis=1, tiled=True)]
    all_to_all x0 -> x1, waiting for transfers between devices: none -> 35.6 us  [swapped_in(): tiles = lax.all_to_all(tiles, axis, split_axis=0, concat_axis=0)]
    another operation x2 -> x4, other arithmetic: 1.19 us -> 10.7 us  [the longest x2 9.51 us: swapped_in(): tiles = jnp.stack([x for _ in range(size)])]
    convert_element_type x2 -> x1, other arithmetic: 23.8 us -> 15.8 us  [adamw(): (master - learn_rate * (update + weight_decay * master)).astype(jnp.bfloa...]
    all_to_all x0 -> x1, starting transfers between devices: none -> 5.91 us  [swapped_in(): tiles = lax.all_to_all(tiles, axis, split_axis=0, concat_axis=0)]
  transfers between devices with their start and end apart: 4 -> 4, of which waited for: 4 -> 4; matrix products, arithmetic and copies ran while one was open for 10% -> 11% of each run, Pallas kernels for 0% -> 0%
where the time goes in v1:
time: 308 us
  waiting for transfers between devices  197 us (64%)
  other arithmetic  32 us (10%)
  matrix products  29.7 us (10%)
  starting transfers between devices  18.9 us (6%)
  local copies, waits for them, and re-layouts  16.6 us (5%)
  between operations  13.5 us (4%)
    all_to_all x1, waiting for transfers between devices, per_device(): lax.all_to_all(results.reshape(src_count, item_count, depth), 'expert', s...  80.5 us
    all_to_all x1, waiting for transfers between devices, per_device(): lax.all_to_all(outgoing, 'expert', split_axis=0, concat_axis=0, tiled=True)  72 us
    all_to_all x1, waiting for transfers between devices, swapped_in(): tiles = lax.all_to_all(tiles, axis, split_axis=0, concat_axis=0)  35.6 us
    dot_general x1, matrix products, expert_apply(): jnp.dot(hidden, down_proj, preferred_element_type=jnp.float32)  16.3 us
    convert_element_type x1, other arithmetic, adamw(): (master - learn_rate * (update + weight_decay * master)).astype(jnp.bfloa...  15.8 us
    dot_general x1, matrix products, expert_apply(): jnp.dot(block_rows, gate_up[0], preferred_element_type=jnp.float32)  10.7 us
    another operation x2, other arithmetic, swapped_in(): tiles = jnp.stack([x for _ in range(size)])  9.51 us
    all_gather x1, waiting for transfers between devices, per_device(): lax.all_gather(gate_up_own, 'dp', axis=2, tiled=True)  9.25 us
  transfers between devices with their start and end apart: 4, of which 4 were waited for; matrix products, arithmetic and copies ran while one was open for 11% of the time, Pallas kernels for 0%

profile of v1, /device:TPU:13, one launch (start us, length us, event | category | flops | bytes accessed | tf_op | source)
XLA Modules:
  0.0 308.1 jit_solution(387371071810607816)
XLA Ops:
  6.5 15.8 %fusion.10 = bf16[1,2,896,1280]{3,2,1,0:T(8,128)(2,1)} fusion(f32[1,2,896,1280]{3,2,1,0:T(8,128)} %param.14, f32[1,2,896,1280]{3,2,1,0:T(8,128)} %param.16, bf16[1,2,896,1280]{3,2,1,0:T(8,128)(2,1)} %param.17, f32[1,2,896,1280]{3,2,1,0:T(8,128)} %param.15), kind=kLoop, calls=%fused_computation.14 | loop fusion | flops 38993920 | bytes 36700160 | tf_op jit(solution)/shard_map/convert_element_type | solution.py:27
  22.4 0.7 copy-done.3
  23.4 1.2 reduce-window.6
  24.6 0.2 slice_reduce_fusion
  24.9 0.6 convert_reduce_fusion
  25.8 5.8 %gather_fusion = bf16[1024,1792]{1,0:T(8,128)(2,1)} fusion(bf16[128,1792]{1,0:T(8,128)(2,1)S(1)} %copy-done, s32[1024]{0:T(1024)S(1)} %broadcast_clamp_fusion), kind=kCustom, calls=%fused_computation | custom fusion | bytes 7344128 | tf_op jit(solution)/shard_map/jit(_take)/gather | solution.py:56
  31.6 4.6 %select_select_fusion = bf16[16,64,1792]{2,1,0:T(8,128)(2,1)} fusion(bf16[16,64,1792]{2,1,0:T(8,128)(2,1)} %bitcast.53, pred[16,64]{1,0:T(8,128)(4,1)S(1)} %compare_and_fusion, pred[16,64]{1,0:T(8,128)(4,1)S(1)} %gt.20), kind=kLoop, calls=%fused_computation.34 | loop fusion | flops 3670016 | bytes 7342080 | tf_op jit(solution)/shard_map/jit(_where)/select_n | solution.py:55
  36.2 6.7 %all-to-all-start = ((bf16[16,64,1792]{2,1,0:T(8,128)(2,1)}), bf16[16,64,1792]{2,1,0:T(8,128)(2,1)}, u32[]{:S(2)}, u32[]{:S(2)}) async-start(bf16[16,64,1792]{2,1,0:T(8,128)(2,1)} %select_select_fusion), calls=%async_computation | async-start | bytes 7340032 | tf_op jit(solution)/shard_map/all_to_all | solution.py:67
  43.0 7.0 %fusion.23 = bf16[1,1,640,1792]{3,2,1,0:T(8,128)(2,1)S(1)} fusion(f32[1,640,1792]{2,1,0:T(8,128)} %param.18, f32[1,640,1792]{2,1,0:T(8,128)} %param.20, bf16[1,640,1792]{2,1,0:T(8,128)(2,1)S(1)} %copy-done.2, f32[1,640,1792]{2,1,0:T(8,128)} %param.19), kind=kLoop, calls=%fused_computation.35 | loop fusion | flops 19496960 | bytes 18350080 | tf_op jit(solution)/shard_map/stack | solution.py:17
  50.0 2.5 pad_maximum_fusion
  52.5 72.0 %all-to-all-done = bf16[16,64,1792]{2,1,0:T(8,128)(2,1)} async-done(((bf16[16,64,1792]{2,1,0:T(8,128)(2,1)}), bf16[16,64,1792]{2,1,0:T(8,128)(2,1)}, u32[]{:S(2)}, u32[]{:S(2)}) %all-to-all-start) | async-done | bytes 3670048 | tf_op jit(solution)/shard_map/all_to_all | solution.py:67
  124.5 5.9 %all-to-all-start.1 = ((bf16[2,1,640,1792]{3,2,1,0:T(8,128)(2,1)}), bf16[2,1,640,1792]{3,2,1,0:T(8,128)(2,1)}, u32[]{:S(2)}, u32[]{:S(2)}) async-start(bf16[2,1,640,1792]{3,2,1,0:T(8,128)(2,1)} %pad_maximum_fusion), calls=%async_computation.1 | async-start | bytes 9175040 | tf_op jit(solution)/shard_map/all_to_all | solution.py:18
  130.4 9.2 %all-gather.2.cloned.1.call-done = bf16[1,2,1792,1280]{3,2,1,0:T(8,128)(2,1)} async-done(((bf16[1,2,896,1280]{3,2,1,0:T(8,128)(2,1)}), bf16[1,2,1792,1280]{3,2,1,0:T(8,128)(2,1)}) %all-gather.2.cloned.1.call-update) | async-done | bytes 9175056 | tf_op jit(solution)/shard_map/all_gather | solution.py:62
  139.6 10.7 %fusion.21 = f32[1024,1280]{1,0:T(8,128)} fusion(bf16[1024,1792]{1,0:T(8,128)(2,1)} %bitcast.4, bf16[1,2,1792,1280]{3,2,1,0:T(8,128)(2,1)} %all-gather.2.cloned.1.call-done), kind=kOutput, calls=%fused_computation.30 | convolution fusion | flops 4697620480 | bytes 13500416 | tf_op jit(solution)/shard_map/dot_general | solution.py:31
  150.3 35.6 %all-to-all-done.1 = bf16[2,1,640,1792]{3,2,1,0:T(8,128)(2,1)} async-done(((bf16[2,1,640,1792]{3,2,1,0:T(8,128)(2,1)}), bf16[2,1,640,1792]{3,2,1,0:T(8,128)(2,1)}, u32[]{:S(2)}, u32[]{:S(2)}) %all-to-all-start.1) | async-done | bytes 4587552 | tf_op jit(solution)/shard_map/all_to_all | solution.py:18
  185.9 16.3 %convolution_convert_fusion = bf16[1024,1792]{1,0:T(8,128)(2,1)} fusion(bf16[1280,1792]{1,0:T(8,128)(2,1)} %bitcast.8, f32[1024,1280]{1,0:T(8,128)} %fusion.21, bf16[1024,1792]{1,0:T(8,128)(2,1)} %bitcast.4, bf16[1,2,1792,1280]{3,2,1,0:T(8,128)(2,1)} %all-gather.2.cloned.1.call-done), kind=kOutput, calls=%fused_computation.33 | convolution fusion | flops 9404940288 | bytes 21757952 | tf_op jit(solution)/shard_map/dot_general | solution.py:34
  202.3 6.2 %all-to-all-start.2 = ((bf16[16,64,1792]{2,1,0:T(8,128)(2,1)}), bf16[16,64,1792]{2,1,0:T(8,128)(2,1)}, u32[]{:S(2)}, u32[]{:S(2)}) async-start(bf16[16,64,1792]{2,1,0:T(8,128)(2,1)} %bitcast.54), calls=%async_computation.2 | async-start | bytes 7340032 | tf_op jit(solution)/shard_map/all_to_all | solution.py:70
  208.6 0.2 copy.27
  209.1 0.1 copy.25
  209.3 80.5 %all-to-all-done.2 = bf16[16,64,1792]{2,1,0:T(8,128)(2,1)} async-done(((bf16[16,64,1792]{2,1,0:T(8,128)(2,1)}), bf16[16,64,1792]{2,1,0:T(8,128)(2,1)}, u32[]{:S(2)}, u32[]{:S(2)}) %all-to-all-start.2) | async-done | bytes 3670048 | tf_op jit(solution)/shard_map/all_to_all | solution.py:70
  289.7 6.5 %gather_fusion.1 = bf16[512,1792]{1,0:T(8,128)(2,1)S(1)} fusion(bf16[1024,1792]{1,0:T(8,128)(2,1)} %bitcast.10, s32[1024]{0:T(1024)S(1)} %pad_clamp_fusion), kind=kCustom, calls=%fused_computation.1 | custom fusion | bytes 3672064 | tf_op jit(solution)/shard_map/jit(_take)/gather | solution.py:78
  296.2 1.5 gather.15
  297.7 2.7 fusion.24
  300.4 0.8 copy.32
  (33 shorter events, 1.1 us)
Async XLA Ops:
  6.5 19.2 %copy-start = (bf16[128,1792]{1,0:T(8,128)(2,1)S(1)}, bf16[128,1792]{1,0:T(8,128)(2,1)}, u32[]{:S(2)}) copy-start(bf16[128,1792]{1,0:T(8,128)(2,1)} %param.11) | copy-start | bytes 1376260
  6.5 133.1 %all-gather.2.cloned.1.call-start = ((), (), s32[]{:S(2)}) async-start(), calls=%async_computation.3 | async-start | bytes 13762560 | tf_op jit(solution)/shard_map/all_gather | solution.py:62
  22.4 0.7 copy-start.3
  36.2 6.7 %copy-start.2 = (bf16[1,640,1792]{2,1,0:T(8,128)(2,1)S(1)}, bf16[1,640,1792]{2,1,0:T(8,128)(2,1)}, u32[]{:S(2)}) copy-start(bf16[1,640,1792]{2,1,0:T(8,128)(2,1)} %param.21) | copy-start | bytes 6881284
  36.2 88.3 %all-to-all-start = ((bf16[16,64,1792]{2,1,0:T(8,128)(2,1)}), bf16[16,64,1792]{2,1,0:T(8,128)(2,1)}, u32[]{:S(2)}, u32[]{:S(2)}) async-start(bf16[16,64,1792]{2,1,0:T(8,128)(2,1)} %select_select_fusion), calls=%async_computation | async-start | bytes 7340032 | tf_op jit(solution)/shard_map/all_to_all | solution.py:67
  124.5 61.5 %all-to-all-start.1 = ((bf16[2,1,640,1792]{3,2,1,0:T(8,128)(2,1)}), bf16[2,1,640,1792]{3,2,1,0:T(8,128)(2,1)}, u32[]{:S(2)}, u32[]{:S(2)}) async-start(bf16[2,1,640,1792]{3,2,1,0:T(8,128)(2,1)} %pad_maximum_fusion), calls=%async_computation.1 | async-start | bytes 9175040 | tf_op jit(solution)/shard_map/all_to_all | solution.py:18
  202.3 6.4 %copy-start.4 = (f32[128,4]{0,1:T(4,128)S(1)}, f32[128,4]{0,1:T(4,128)}, u32[]{:S(2)}) copy-start(f32[128,4]{0,1:T(4,128)} %param.13) | copy-start | bytes 6148
  202.3 87.5 %all-to-all-start.2 = ((bf16[16,64,1792]{2,1,0:T(8,128)(2,1)}), bf16[16,64,1792]{2,1,0:T(8,128)(2,1)}, u32[]{:S(2)}, u32[]{:S(2)}) async-start(bf16[16,64,1792]{2,1,0:T(8,128)(2,1)} %bitcast.54), calls=%async_computation.2 | async-start | bytes 7340032 | tf_op jit(solution)/shard_map/all_to_all | solution.py:70
  296.2 5.0 %copy-start.1 = (bf16[128,1792]{1,0:T(8,128)(2,1)S(1)}, bf16[128,1792]{1,0:T(8,128)(2,1)}, u32[]{:S(2)}) copy-start(bf16[128,1792]{1,0:T(8,128)(2,1)} %param.11) | copy-start | bytes 1376260
Sparse Core Ops, SparseCore 0:
  22.5 117.0 all-gather.1
